TPU v7x, 32 devices: a whole 2x2x4 slice. The times are simulated.
32 devices in a mesh: row: 4 (over y, x), col: 8 (over z, core).
Axes of the slice: x: 2, y: 2, z: 4, core: 2. Of those that a mesh axis runs over, the one named last changes fastest.
Arguments:
- root_inverse: float32 [12288, 12288], P('row', 'col'), may hold values from -6 to 6, as said below
- panel_root: float32 [2, 12288, 256], P(None, ('row', 'col')), may hold values from -0.0546875 to 0.0546875
- panel_tail: float32 [1, 256, 256], replicated, may hold values from -0.375 to 0.375
- factor_inverse: float32 [2, 256, 256], replicated, may hold values from -1 to 2, as said below
- ancestors: int32 [84], replicated, may hold values from 0 to 95, as said below
Outputs:
- border: float32 [2, 12288, 256], P(None, ('row', 'col'))
- border_tail: float32 [1, 256, 256], replicated
- diagonal: float32 [2, 256, 256], replicated
Inputs may be any that keep to these rules, and one draw needn't show every extreme that they name: `ancestors`: each of the two lists is increasing and holds distinct root blocks; the list of supernode 1 is a subset of that of supernode 0. `factor_inverse`: each block is lower triangular with a positive diagonal. `root_inverse`: the matrix is symmetric.
All inputs are finite; a program needn't handle non-finite values.
Results may differ from a plain program's by a relative error of at most 0.0001.
Values sent between devices are 32-bit elements; how exact they have to be, the bound alone decides.
No kernel may reach another device: no remote copies, remote signals or barrier semaphores. Data moves between devices by JAX's collectives and lax.ppermute only.
A program may use at most 64 MiB of HBM per device.

v0:
```python
import jax
import jax.numpy as jnp
from jax import lax
from jax.sharding import PartitionSpec as P

R = 12288
BLK = 128


def from_root(x, axis, root):
    mine = lax.axis_index(axis) == root
    return lax.psum(jnp.where(mine, x, jnp.zeros_like(x)), axis)


def product(left, right):
    return jnp.dot(left, right, precision=lax.Precision.HIGHEST, preferred_element_type=jnp.float32)


def tail_slot(later, earlier):
    return later * (later - 1) // 2 + earlier


def member(start, count, listed):
    block_ids = (start + lax.iota(jnp.int32, count)) // BLK
    return jnp.any(block_ids[:, None] == listed[None, :], axis=1).astype(jnp.float32)[:, None]


def local(root_inverse, panel_root, panel_tail, factor_inverse, ancestors):
    row_index = lax.axis_index("row")
    col_index = lax.axis_index("col")
    share = panel_root.shape[1]
    block_rows = root_inverse.shape[0]
    col_rows = root_inverse.shape[1]
    share_start = row_index * block_rows + col_index * share
    nblocks = R // BLK
    counts = [nblocks // 2, 3 * nblocks // 8]
    lists = []
    start = 0
    for node in range(2):
        lists.append(ancestors[start : start + counts[node]])
        start = start + counts[node]
    borders = []
    diagonals = []
    tails = [None]
    for node in range(2):
        listed = lists[node]
        gathered = lax.all_gather(panel_root[node : node + 1], "col", axis=1, tiled=True)
        owner = col_index * col_rows // block_rows
        offset = col_index * col_rows - owner * block_rows
        column_part = lax.dynamic_slice_in_dim(gathered, offset, col_rows, 1)
        column_part = from_root(column_part, "row", owner)
        col_start = col_index * col_rows
        joined = [column_part[0] * member(col_start, col_rows, [listed][0])][0]
        images = lax.psum_scatter(
            product(root_inverse, joined), "col", scatter_dimension=0, tiled=True
        )
        image = [images][0]
        mask = member(share_start, share, listed)
        panel = panel_root[node] * mask
        for prior in range(node):
            image = image + product(borders[prior], panel_tail[tail_slot(node, prior)])
        crossing = [product(borders[prior].T, panel) for prior in range(node)]
        carried = []
        for prior in range(node):
            value = product(diagonals[prior], panel_tail[tail_slot(node, 0)])
            carried.append(value)
        own_part = product(panel.T, image)
        base = product(factor_inverse[node].T, factor_inverse[node])
        cross = []
        joint = own_part
        for prior in range(node):
            joint = joint + product(panel_tail[tail_slot(node, prior)].T, crossing[prior])
        totals = lax.psum(tuple([joint] + crossing), ("row", "col"))
        block = base + totals[0]
        for prior in range(node):
            cross.append(totals[1 + prior] + carried[prior])
            block = block + product(panel_tail[tail_slot(node, prior)].T, carried[prior])
        for prior in range(node):
            tails[tail_slot(node, prior)] = -cross[prior]
        borders.append(-(mask * image))
        diagonals.append(block)
    return (jnp.stack(borders), jnp.stack(tails), jnp.stack(diagonals))


def solution(mesh):
    placed = (P("row", "col"), P(None, ("row", "col"), None), P(), P(), P())
    return jax.shard_map(
        local,
        mesh=mesh,
        in_specs=placed,
        out_specs=(P(None, ("row", "col"), None), P(), P()),
        check_vma=False,
    )
```

profile of v0, /device:TPU:0, one launch (start us, length us, event | category | flops | bytes accessed | tf_op | source)
XLA Modules:
  0.0 430.4 jit_solution(5512054418208885752)
XLA Ops:
  7.2 1.2 fusion.31
  8.4 0.9 copy.23
  9.4 0.9 copy.24
  10.4 40.7 %all-gather.3.cloned.1.call-done = f32[1,3072,256]{1,2,0:T(8,128)} async-done(((f32[1,384,256]{1,2,0:T(8,128)}), f32[1,3072,256]{1,2,0:T(8,128)}) %all-gather.3.cloned.1.call-update) | async-done | bytes 3145744 | tf_op jit(solution)/shard_map/all_gather | solution.py:47
  51.1 2.7 select_bitcast_fusion.1
  53.8 36.7 %all-gather.5.cloned.1.call-done = f32[1,3072,256]{1,2,0:T(8,128)} async-done(((f32[1,384,256]{1,2,0:T(8,128)}), f32[1,3072,256]{1,2,0:T(8,128)}) %all-gather.5.cloned.1.call-update) | async-done | bytes 3145744 | tf_op jit(solution)/shard_map/all_gather | solution.py:47
  90.5 2.7 select_bitcast_fusion
  93.3 0.6 copy-done.9
  93.9 0.1 compare_reduce_fusion
  94.0 85.5 %all-reduce.7.cloned.1.call-done = (f32[1536,256]{0,1:T(8,128)}, f32[1536,256]{0,1:T(8,128)}) async-done(((f32[1536,256]{0,1:T(8,128)}, f32[1536,256]{0,1:T(8,128)}), (f32[1536,256]{0,1:T(8,128)}, f32[1536,256]{0,1:T(8,128)})) %all-reduce.7.cloned.1.call-update) | async-done | bytes 3145744 | tf_op jit(solution)/shard_map/psum | solution.py:12
  179.5 20.6 %convolution_bitcast_fusion.1 = f32[3072,256]{0,1:T(8,128)} fusion(f32[3072,1536]{1,0:T(8,128)} %param.5, f32[1536,256]{0,1:T(8,128)} %get-tuple-element.13, f32[1536]{0:T(1024)S(1)} %convert_element_type.29), kind=kOutput, calls=%fused_computation.1 | convolution fusion | flops 14495907840 | bytes 23599104 | tf_op jit(solution)/shard_map/dot_general | solution.py:16
  200.2 0.1 compare_reduce_fusion.1
  200.3 1.1 copy-done.4
  201.5 20.1 %convolution_bitcast_fusion = f32[3072,256]{0,1:T(8,128)} fusion(f32[3072,1536]{1,0:T(8,128)} %param.5, f32[1536,256]{0,1:T(8,128)S(1)} %copy-done.4, f32[1536]{0:T(1024)S(1)} %convert_element_type.31), kind=kOutput, calls=%fused_computation | convolution fusion | flops 14495907840 | bytes 23599104 | tf_op jit(solution)/shard_map/dot_general | solution.py:16
  221.7 0.2 all-reduce.5.cloned.1.call-start
  221.9 0.1 compare_reduce_fusion.2
  222.0 0.1 compare_reduce_fusion.3
  222.1 18.5 %reduce-scatter.3.cloned.1.call-done = f32[384,256]{0,1:T(8,128)} async-done(((f32[3072,256]{0,1:T(8,128)}), f32[384,256]{0,1:T(8,128)}) %reduce-scatter.3.cloned.1.call-update) | async-done | bytes 393232 | tf_op jit(solution)/shard_map/reduce_scatter | solution.py:54
  240.6 41.8 %reduce-scatter.5.cloned.1.call-done = f32[384,256]{0,1:T(8,128)} async-done(((f32[3072,256]{0,1:T(8,128)}), f32[384,256]{0,1:T(8,128)}) %reduce-scatter.5.cloned.1.call-update) | async-done | bytes 393232 | tf_op jit(solution)/shard_map/reduce_scatter | solution.py:54
  282.5 1.8 convolution_add_fusion
  284.2 0.6 fusion.8
  284.9 0.6 fusion.9
  285.5 1.3 fusion.4
  286.8 1.3 fusion.7
  288.3 1.1 copy.19
  289.5 129.3 %all-reduce.5.cloned.1.call-done = (f32[256,256]{1,0:T(8,128)}, f32[256,256]{1,0:T(8,128)}, f32[256,256]{1,0:T(8,128)}) async-done(((f32[256,256]{1,0:T(8,128)}, f32[256,256]{1,0:T(8,128)}, f32[256,256]{1,0:T(8,128)}), (f32[256,256]{1,0:T(8,128)}, f32[256,256]{1,0:T(8,128)}, f32[256,256]{1,0:T(8,128)})) %all-reduce.5.cloned.1.call-update) | async-done | bytes 786448 | tf_op jit(solution)/shard_map/psum | solution.py:73
  418.7 1.6 convolution_add_fusion.2
  420.3 0.4 fusion.15
  420.7 0.6 convolution_add_fusion.1
  421.3 0.6 fusion.3
  422.0 0.7 negate_bitcast_fusion.1
  422.7 0.8 pad_maximum_fusion.1
  (39 shorter events, 0.6 us)
Async XLA Ops:
  7.2 275.3 %copy-start = (f32[1,256,256]{2,1,0:T(8,128)S(1)}, f32[1,256,256]{2,1,0:T(8,128)}, u32[]{:S(2)}) copy-start(f32[1,256,256]{2,1,0:T(8,128)} %param.7) | copy-start | bytes 786436
  7.2 44.0 %all-gather.3.cloned.1.call-start = ((), (), s32[]{:S(2)}) async-start(), calls=%async_computation.2 | async-start | bytes 3538944 | tf_op jit(solution)/shard_map/all_gather | solution.py:47
  9.4 81.1 %all-gather.5.cloned.1.call-start = ((), (), s32[]{:S(2)}) async-start(), calls=%async_computation.4 | async-start | bytes 3538944 | tf_op jit(solution)/shard_map/all_gather | solution.py:47
  10.4 169.1 %all-reduce.7.cloned.1.call-start = ((), (), s32[]{:S(2)}) async-start(), calls=%async_computation.7 | async-start | bytes 6291456 | tf_op jit(solution)/shard_map/psum | solution.py:12
  93.2 0.7 copy-start.9
  93.2 147.4 %reduce-scatter.3.cloned.1.call-start = ((), (), s32[]{:S(2)}) async-start(), calls=%async_computation.3 | async-start | bytes 3538944 | tf_op jit(solution)/shard_map/reduce_scatter | solution.py:54
  200.1 1.4 copy-start.4
  200.1 82.4 %reduce-scatter.5.cloned.1.call-start = ((), (), s32[]{:S(2)}) async-start(), calls=%async_computation.5 | async-start | bytes 3538944 | tf_op jit(solution)/shard_map/reduce_scatter | solution.py:54
  221.6 62.6 %copy-start.1 = (f32[1,384,256]{1,2,0:T(8,128)S(1)}, f32[1,384,256]{1,2,0:T(8,128)}, u32[]{:S(2)}) copy-start(f32[1,384,256]{1,2,0:T(8,128)} %copy.24) | copy-start | bytes 1179652
  221.7 197.1 %all-reduce.5.cloned.1.call-start = ((), (), s32[]{:S(2)}) async-start(), calls=%async_computation.6 | async-start | bytes 1572864 | tf_op jit(solution)/shard_map/psum | solution.py:73
  240.6 44.2 %copy-start.2 = (f32[384,256]{0,1:T(8,128)S(1)}, f32[384,256]{0,1:T(8,128)}, u32[]{:S(2)}) copy-start(f32[384,256]{0,1:T(8,128)} %reduce-scatter.3.cloned.1.call-done) | copy-start | bytes 1179652
  284.2 2.6 copy-start.3
  285.5 2.6 copy-start.5
  288.2 130.5 %copy-start.6 = (f32[2,256,256]{2,1,0:T(8,128)S(1)}, f32[2,256,256]{2,1,0:T(8,128)}, u32[]{:S(2)}) copy-start(f32[2,256,256]{2,1,0:T(8,128)} %param.8) | copy-start | bytes 1572868
  418.7 2.0 copy-start.8
  418.7 3.2 copy-start.7
Sparse Core Ops, SparseCore 0:
  10.2 40.9 all-gather.2
  53.3 37.1 all-gather.4
  93.6 85.8 all-reduce.6
  200.2 40.3 reduce-scatter.2
  242.8 39.6 reduce-scatter.4
  288.4 130.2 all-reduce.4
where the time goes:
time: 431 us; the launch traced here: 430 us
  waiting for transfers between devices  353 us (82%)
  matrix products  49.5 us (11%)
  between operations  14.3 us (3%)
  other arithmetic  7.57 us (2%)
  local copies, waits for them, and re-layouts  5.99 us (1%)
    psum x1, waiting for transfers between devices, local(): totals = lax.psum(tuple([joint] + crossing), ('row', 'col'))  129 us
    psum x1, waiting for transfers between devices, from_root(): return lax.psum(jnp.where(mine, x, jnp.zeros_like(x)), axis)  85.5 us
    all_gather x2, waiting for transfers between devices, local(): lax.all_gather(panel_root[node:node + 1], 'col', axis=1, tiled=True)  77.4 us
    reduce_scatter x2, waiting for transfers between devices, local(): lax.psum_scatter(product(root_inverse, joined), 'col', scatter_dimension=...  60.3 us
    dot_general x11, matrix products, product(): jnp.dot(left, right, precision=lax.Precision.HIGHEST, preferred_element_t...  49.5 us
  transfers between devices with their start and end apart: 6, of which 6 were waited for; matrix products, arithmetic and copies ran while one was open for 6% of the time, Pallas kernels for 0%

commit v1 on v0

--- a/solution.py
+++ b/solution.py
@@ -70,7 +70,7 @@
         joint = own_part
         for prior in range(node):
             joint = joint + product(panel_tail[tail_slot(node, prior)].T, crossing[prior])
-        totals = lax.psum(tuple([joint] + crossing), ("row", "col"))
+        totals = lax.psum(lax.psum(tuple([joint] + crossing), "row"), "col")
         block = base + totals[0]
         for prior in range(node):
             cross.append(totals[1 + prior] + carried[prior])

time: 431 us -> 409 us (0.949)
  waiting for transfers between devices: 353 us -> 330 us
    psum x1 -> x2, waiting for transfers between devices: 129 us -> 107 us  [local(): totals = lax.psum(lax.psum(tuple([joint] + crossing), 'row'), 'col')]
  transfers between devices with their start and end apart: 6 -> 7, of which waited for: 6 -> 7; matrix products, arithmetic and copies ran while one was open for 6% -> 6% of each run, Pallas kernels for 0% -> 0%
where the time goes in v1:
time: 409 us; the launch traced here: 408 us
  waiting for transfers between devices  330 us (81%)
  matrix products  49.5 us (12%)
  between operations  14.3 us (3%)
  other arithmetic  7.59 us (2%)
  local copies, waits for them, and re-layouts  5.99 us (1%)
    psum x2, waiting for transfers between devices, local(): totals = lax.psum(lax.psum(tuple([joint] + crossing), 'row'), 'col')  107 us
    psum x1, waiting for transfers between devices, from_root(): return lax.psum(jnp.where(mine, x, jnp.zeros_like(x)), axis)  85.5 us
    all_gather x2, waiting for transfers between devices, local(): lax.all_gather(panel_root[node:node + 1], 'col', axis=1, tiled=True)  77.3 us
    reduce_scatter x2, waiting for transfers between devices, local(): lax.psum_scatter(product(root_inverse, joined), 'col', scatter_dimension=...  60.2 us
    dot_general x11, matrix products, product(): jnp.dot(left, right, precision=lax.Precision.HIGHEST, preferred_element_t...  49.5 us
  transfers between devices with their start and end apart: 7, of which 7 were waited for; matrix products, arithmetic and copies ran while one was open for 6% of the time, Pallas kernels for 0%

profile of v1, /device:TPU:0, one launch (start us, length us, event | category | flops | bytes accessed | tf_op | source)
XLA Modules:
  0.0 408.4 jit_solution(7654089796905550173)
XLA Ops:
  7.2 1.2 fusion.31
  8.4 0.9 copy.23
  9.4 0.9 copy.24
  10.4 40.7 %all-gather.3.cloned.1.call-done = f32[1,3072,256]{1,2,0:T(8,128)} async-done(((f32[1,384,256]{1,2,0:T(8,128)}), f32[1,3072,256]{1,2,0:T(8,128)}) %all-gather.3.cloned.1.call-update) | async-done | bytes 3145744 | tf_op jit(solution)/shard_map/all_gather | solution.py:47
  51.1 2.7 select_bitcast_fusion.1
  53.8 36.7 %all-gather.5.cloned.1.call-done = f32[1,3072,256]{1,2,0:T(8,128)} async-done(((f32[1,384,256]{1,2,0:T(8,128)}), f32[1,3072,256]{1,2,0:T(8,128)}) %all-gather.5.cloned.1.call-update) | async-done | bytes 3145744 | tf_op jit(solution)/shard_map/all_gather | solution.py:47
  90.5 2.8 select_bitcast_fusion
  93.3 0.6 copy-done.9
  93.9 0.1 compare_reduce_fusion
  94.0 85.5 %all-reduce.11.cloned.1.call-done = (f32[1536,256]{0,1:T(8,128)}, f32[1536,256]{0,1:T(8,128)}) async-done(((f32[1536,256]{0,1:T(8,128)}, f32[1536,256]{0,1:T(8,128)}), (f32[1536,256]{0,1:T(8,128)}, f32[1536,256]{0,1:T(8,128)})) %all-reduce.11.cloned.1.call-update) | async-done | bytes 3145744 | tf_op jit(solution)/shard_map/psum | solution.py:12
  179.5 20.6 %convolution_bitcast_fusion.1 = f32[3072,256]{0,1:T(8,128)} fusion(f32[3072,1536]{1,0:T(8,128)} %param.5, f32[1536,256]{0,1:T(8,128)} %get-tuple-element.16, f32[1536]{0:T(1024)S(1)} %convert_element_type.29), kind=kOutput, calls=%fused_computation.1 | convolution fusion | flops 14495907840 | bytes 23599104 | tf_op jit(solution)/shard_map/dot_general | solution.py:16
  200.2 0.1 compare_reduce_fusion.1
  200.3 1.1 copy-done.4
  201.5 20.1 %convolution_bitcast_fusion = f32[3072,256]{0,1:T(8,128)} fusion(f32[3072,1536]{1,0:T(8,128)} %param.5, f32[1536,256]{0,1:T(8,128)S(1)} %copy-done.4, f32[1536]{0:T(1024)S(1)} %convert_element_type.31), kind=kOutput, calls=%fused_computation | convolution fusion | flops 14495907840 | bytes 23599104 | tf_op jit(solution)/shard_map/dot_general | solution.py:16
  221.6 0.2 all-reduce.9.cloned.1.call-start
  221.9 0.1 compare_reduce_fusion.2
  222.1 18.5 %reduce-scatter.3.cloned.1.call-done = f32[384,256]{0,1:T(8,128)} async-done(((f32[3072,256]{0,1:T(8,128)}), f32[384,256]{0,1:T(8,128)}) %reduce-scatter.3.cloned.1.call-update) | async-done | bytes 393232 | tf_op jit(solution)/shard_map/reduce_scatter | solution.py:54
  240.6 41.7 %reduce-scatter.5.cloned.1.call-done = f32[384,256]{0,1:T(8,128)} async-done(((f32[3072,256]{0,1:T(8,128)}), f32[384,256]{0,1:T(8,128)}) %reduce-scatter.5.cloned.1.call-update) | async-done | bytes 393232 | tf_op jit(solution)/shard_map/reduce_scatter | solution.py:54
  282.3 1.8 convolution_add_fusion
  284.1 0.6 fusion.8
  284.8 0.6 fusion.9
  285.4 1.3 fusion.4
  286.7 1.3 fusion.7
  288.1 48.1 %all-reduce.9.cloned.1.call-done = (f32[256,256]{1,0:T(8,128)}, f32[256,256]{1,0:T(8,128)}, f32[256,256]{1,0:T(8,128)}) async-done(((f32[256,256]{1,0:T(8,128)}, f32[256,256]{1,0:T(8,128)}, f32[256,256]{1,0:T(8,128)}), (f32[256,256]{1,0:T(8,128)}, f32[256,256]{1,0:T(8,128)}, f32[256,256]{1,0:T(8,128)})) %all-reduce.9.cloned.1.call-update) | async-done | bytes 786448 | tf_op jit(solution)/shard_map/psum | solution.py:73
  336.4 1.1 copy.19
  337.6 59.2 %all-reduce.7.cloned.1.call-done = (f32[256,256]{1,0:T(8,128)}, f32[256,256]{1,0:T(8,128)}, f32[256,256]{1,0:T(8,128)}) async-done(((f32[256,256]{1,0:T(8,128)}, f32[256,256]{1,0:T(8,128)}, f32[256,256]{1,0:T(8,128)}), (f32[256,256]{1,0:T(8,128)}, f32[256,256]{1,0:T(8,128)}, f32[256,256]{1,0:T(8,128)})) %all-reduce.7.cloned.1.call-update) | async-done | bytes 786448 | tf_op jit(solution)/shard_map/psum | solution.py:73
  396.8 1.6 convolution_add_fusion.2
  398.4 0.4 fusion.15
  398.8 0.6 convolution_add_fusion.1
  399.4 0.6 fusion.3
  400.0 0.7 negate_bitcast_fusion.1
  400.7 0.8 pad_maximum_fusion.1
  (42 shorter events, 0.7 us)
Async XLA Ops:
  7.2 275.2 %copy-start = (f32[1,256,256]{2,1,0:T(8,128)S(1)}, f32[1,256,256]{2,1,0:T(8,128)}, u32[]{:S(2)}) copy-start(f32[1,256,256]{2,1,0:T(8,128)} %param.7) | copy-start | bytes 786436
  7.2 44.0 %all-gather.3.cloned.1.call-start = ((), (), s32[]{:S(2)}) async-start(), calls=%async_computation.2 | async-start | bytes 3538944 | tf_op jit(solution)/shard_map/all_gather | solution.py:47
  9.4 81.1 %all-gather.5.cloned.1.call-start = ((), (), s32[]{:S(2)}) async-start(), calls=%async_computation.4 | async-start | bytes 3538944 | tf_op jit(solution)/shard_map/all_gather | solution.py:47
  10.4 169.1 %all-reduce.11.cloned.1.call-start = ((), (), s32[]{:S(2)}) async-start(), calls=%async_computation.8 | async-start | bytes 6291456 | tf_op jit(solution)/shard_map/psum | solution.py:12
  93.2 0.7 copy-start.9
  93.2 147.4 %reduce-scatter.3.cloned.1.call-start = ((), (), s32[]{:S(2)}) async-start(), calls=%async_computation.3 | async-start | bytes 3538944 | tf_op jit(solution)/shard_map/reduce_scatter | solution.py:54
  200.1 1.4 copy-start.4
  200.1 82.2 %reduce-scatter.5.cloned.1.call-start = ((), (), s32[]{:S(2)}) async-start(), calls=%async_computation.5 | async-start | bytes 3538944 | tf_op jit(solution)/shard_map/reduce_scatter | solution.py:54
  221.6 62.5 %copy-start.1 = (f32[1,384,256]{1,2,0:T(8,128)S(1)}, f32[1,384,256]{1,2,0:T(8,128)}, u32[]{:S(2)}) copy-start(f32[1,384,256]{1,2,0:T(8,128)} %copy.24) | copy-start | bytes 1179652
  221.6 114.6 %all-reduce.9.cloned.1.call-start = ((), (), s32[]{:S(2)}) async-start(), calls=%async_computation.7 | async-start | bytes 1572864 | tf_op jit(solution)/shard_map/psum | solution.py:73
  240.6 44.1 %copy-start.2 = (f32[384,256]{0,1:T(8,128)S(1)}, f32[384,256]{0,1:T(8,128)}, u32[]{:S(2)}) copy-start(f32[384,256]{0,1:T(8,128)} %reduce-scatter.3.cloned.1.call-done) | copy-start | bytes 1179652
  284.1 2.6 copy-start.3
  285.4 2.6 copy-start.5
  288.0 108.7 %all-reduce.7.cloned.1.call-start = ((), (), s32[]{:S(2)}) async-start(), calls=%async_computation.6 | async-start | bytes 1572864 | tf_op jit(solution)/shard_map/psum | solution.py:73
  336.3 60.4 %copy-start.6 = (f32[2,256,256]{2,1,0:T(8,128)S(1)}, f32[2,256,256]{2,1,0:T(8,128)}, u32[]{:S(2)}) copy-start(f32[2,256,256]{2,1,0:T(8,128)} %param.8) | copy-start | bytes 1572868
  396.8 2.0 copy-start.8
  396.8 3.2 copy-start.7
Sparse Core Ops, SparseCore 0:
  10.2 40.9 all-gather.2
  53.3 37.1 all-gather.4
  93.6 85.8 all-reduce.10
  200.2 40.3 reduce-scatter.2
  242.8 39.5 reduce-scatter.4
  288.2 48.0 all-reduce.8
  338.8 57.9 all-reduce.6
